TPU v7x, 32 devices: a whole 2x2x4 slice. The times are simulated.
32 devices in a mesh: dp: 4 (over y, x), ctx: 8 (over z, core).
Axes of the slice: x: 2, y: 2, z: 4, core: 2. Of those that a mesh axis runs over, the one named last changes fastest.
Arguments:
- query_rows: bfloat16 [4, 1024, 1024], P('dp', 'ctx'), may hold values from -0.59765625 to 0.59765625
- key_rows: bfloat16 [4, 1024, 1024], P('dp', 'ctx'), may hold values from -0.59765625 to 0.59765625
- value_rows: bfloat16 [4, 1024, 2048], P('dp', 'ctx'), may hold values from -6 to 6
- log_decay: bfloat16 [4, 1024, 1024], P('dp', 'ctx'), may hold values from -1 to 0, as said below
- out_grad: bfloat16 [4, 1024, 2048], P('dp', 'ctx'), may hold values from -1.796875 to 1.796875
- doc_ids: int32 [4, 1024], P('dp', 'ctx'), may hold values from 0 to 3, as said below
- block_order: int32 [4, 8, 4], P(None, 'ctx'), may hold values from 0 to 3, each once within a row
Outputs:
- attn_out: bfloat16 [4, 1024, 2048], P('dp', 'ctx')
- query_grad: bfloat16 [4, 1024, 1024], P('dp', 'ctx')
- key_grad: bfloat16 [4, 1024, 1024], P('dp', 'ctx')
- value_grad: bfloat16 [4, 1024, 2048], P('dp', 'ctx')
- decay_grad: bfloat16 [4, 1024, 1024], P('dp', 'ctx')
Inputs may be any that keep to these rules, and one draw needn't show every extreme that they name: `log_decay`: nonpositive. `doc_ids`: never falls along a pack; every document number of a pack is used; each document has 1 to 512 positions, one of them exactly 512 and one 8 or fewer. `block_order`: each row of a device's list names each of its 4 blocks once.
All inputs are finite; a program needn't handle non-finite values.
Results may differ from a plain program's by a relative error of at most 0.0015.
Values may be sent and summed in bfloat16 or wider, within the bound.
A program may use at most 192 MiB of HBM per device.

v0:
```python
import jax
import jax.numpy as jnp
from jax import lax
from jax.sharding import PartitionSpec as P

DK = 64
DV = 128
BLK = 32
HIGH = lax.Precision.HIGHEST


def prefix(part, axis, combine, identity, reverse):
    count = lax.axis_size(axis)
    place = lax.axis_index(axis)
    ahead = count - 1 - place if reverse else place
    gathered = jax.tree.map(lambda a: lax.all_gather(a, axis), part)
    state = jax.tree.map(lambda a, e: jnp.zeros_like(a) + jnp.asarray(e, a.dtype), part, identity)

    def one(hop, state):
        source = count - 1 - hop if reverse else hop
        return combine(
            state, jax.tree.map(lambda a: lax.dynamic_index_in_dim(a, source, 0, False), gathered)
        )

    return lax.fori_loop(0, ahead, one, state)


def prepare(query_b, key_b, value_b, decay_b, doc_row):
    row_count = query_b.shape[0]
    head_count = query_b.shape[1] // DK
    query_f = query_b.astype(jnp.float32).reshape(row_count, head_count, DK)
    key_f = key_b.astype(jnp.float32).reshape(row_count, head_count, DK)
    value_f = value_b.astype(jnp.float32).reshape(row_count, head_count, DV)
    cumul = jnp.cumsum(decay_b.astype(jnp.float32).reshape(row_count, head_count, DK), axis=0)
    total_log = cumul[-1]
    growth = jnp.exp(cumul)
    shrink = jnp.exp(-cumul)
    to_end = jnp.exp(total_log[None] - cumul)
    later_pos = lax.broadcasted_iota(jnp.int32, (row_count, row_count), 0)
    earlier_pos = lax.broadcasted_iota(jnp.int32, (row_count, row_count), 1)
    same_doc = ((later_pos >= earlier_pos) & (doc_row[:, None] == doc_row[None, :])).astype(
        jnp.float32
    )
    first_id = doc_row[0]
    last_id = doc_row[-1]
    in_first = (doc_row == first_id).astype(jnp.float32)[:, None, None]
    in_last = (doc_row == last_id).astype(jnp.float32)[:, None, None]
    query_t = query_f * growth
    key_t = key_f * shrink
    scores = jnp.einsum("thi,shi->hts", query_t, key_t, precision=HIGH) * same_doc[None]
    return {
        "query_f": query_f,
        "key_f": key_f,
        "value_f": value_f,
        "growth": growth,
        "shrink": shrink,
        "to_end": to_end,
        "same_doc": same_doc,
        "first_id": first_id,
        "last_id": last_id,
        "in_first": in_first,
        "in_last": in_last,
        "query_t": query_t,
        "key_t": key_t,
        "scores": scores,
        "decay_all": jnp.exp(total_log),
    }


def state_end(parts):
    return jnp.einsum(
        "shi,shj->hij",
        parts["key_f"] * parts["to_end"] * parts["in_last"],
        parts["value_f"],
        precision=HIGH,
    )


def start_grad(parts, grad_f):
    factor = DK ** (-0.5)
    return factor * jnp.einsum(
        "thi,thj->hij", parts["query_t"] * parts["in_first"], grad_f, precision=HIGH
    )


def finish(parts, grad_f, state_in, use_state, carry_in, use_carry):
    factor = DK ** (-0.5)
    head_w = parts["in_first"] * use_state
    tail_w = parts["in_last"] * use_carry
    attn_rows = factor * (
        jnp.einsum("hts,shj->thj", parts["scores"], parts["value_f"], precision=HIGH)
        + jnp.einsum("thi,hij->thj", parts["query_t"], state_in, precision=HIGH) * head_w
    )
    grad_scores = (
        jnp.einsum("thj,shj->hts", grad_f, parts["value_f"], precision=HIGH)
        * parts["same_doc"][None]
    )
    grad_query = (
        factor
        * parts["growth"]
        * (
            jnp.einsum("hts,shi->thi", grad_scores, parts["key_t"], precision=HIGH)
            + jnp.einsum("thj,hij->thi", grad_f, state_in, precision=HIGH) * head_w
        )
    )
    grad_value = (
        factor * jnp.einsum("hts,thj->shj", parts["scores"], grad_f, precision=HIGH)
        + jnp.einsum("shi,hij->shj", parts["key_f"] * parts["to_end"], carry_in, precision=HIGH)
        * tail_w
    )
    grad_key = (
        factor
        * parts["shrink"]
        * jnp.einsum("hts,thi->shi", grad_scores, parts["query_t"], precision=HIGH)
        + parts["to_end"]
        * jnp.einsum("hij,shj->shi", carry_in, parts["value_f"], precision=HIGH)
        * tail_w
    )
    grad_log = parts["query_f"] * grad_query - parts["key_f"] * grad_key
    sum_start = jnp.sum(grad_log * parts["in_first"], axis=0)
    return (attn_rows, grad_query, grad_key, grad_value, grad_log, sum_start)


def decay_grad_of(parts, grad_log, sums_in, use_carry):
    inside = jnp.einsum("ts,thi->shi", parts["same_doc"], grad_log, precision=HIGH)
    return inside + sums_in[None] * parts["in_last"] * use_carry


def select_tree(flag, yes_tree, no_tree):
    return tuple((jnp.where(flag, left, right) for left, right in zip(yes_tree, no_tree)))


def join_forward(before, follow):
    b_dec, b_state, b_first, b_last = before
    f_dec, f_state, f_first, f_last = follow
    joined = ((f_first == f_last) & (b_last == f_first)).astype(jnp.float32)
    merged = (
        f_dec * (joined * b_dec + 1.0 - joined),
        f_state + joined * f_dec[..., None] * b_state,
        b_first,
        f_last,
    )
    return select_tree(b_first < 0, follow, select_tree(f_first < 0, before, merged))


def join_backward(before, follow):
    b_dec, b_state, b_first, b_last = before
    f_dec, f_state, f_first, f_last = follow
    joined = ((f_first == f_last) & (f_last == b_first)).astype(jnp.float32)
    merged = (
        f_dec * (joined * b_dec + 1.0 - joined),
        f_state + joined * f_dec[..., None] * b_state,
        f_first,
        b_last,
    )
    return select_tree(b_first < 0, follow, select_tree(f_first < 0, before, merged))


def join_sums(before, follow):
    b_sum, b_first, b_last = before
    f_sum, f_first, f_last = follow
    joined = ((f_first == f_last) & (f_last == b_first)).astype(jnp.float32)
    merged = (f_sum + joined * b_sum, f_first, b_last)
    return select_tree(b_first < 0, follow, select_tree(f_first < 0, before, merged))


def inverse_of(order_lists):
    block_count = order_lists.shape[-1]
    slot_ids = jnp.arange(block_count, dtype=jnp.int32)
    matches = order_lists[..., :, None] == slot_ids
    return jnp.sum(jnp.where(matches, slot_ids[:, None], 0), axis=-2)


def body(query_rows, key_rows, value_rows, log_decay, out_grad, doc_ids, block_order):
    dp_count = lax.axis_size("dp")
    dp_index = lax.axis_index("dp")
    row_count = query_rows.shape[1]
    block_count = row_count // BLK
    per_peer = block_count // dp_count
    order_lists = block_order[:, 0, :]
    my_order = order_lists[dp_index]
    gathered = (
        lax.all_gather(query_rows, "dp", axis=0, tiled=True),
        lax.all_gather(key_rows, "dp", axis=0, tiled=True),
        lax.all_gather(value_rows, "dp", axis=0, tiled=True),
        lax.all_gather(log_decay, "dp", axis=0, tiled=True),
    )
    inverse = inverse_of(order_lists)
    wanted = dp_index * per_peer + jnp.arange(per_peer, dtype=jnp.int32)
    slot_ids = inverse[:, wanted]
    source_ids = jnp.arange(dp_count, dtype=jnp.int32)[:, None]
    balanced = tuple(
        (
            whole.reshape(dp_count, block_count, BLK, whole.shape[-1])[
                source_ids, slot_ids
            ].reshape(row_count, whole.shape[-1])
            for whole in gathered
        )
    )
    query_bal, key_bal, value_bal, decay_bal = balanced
    doc_row = doc_ids[0]
    parts = prepare(query_bal, key_bal, value_bal, decay_bal, doc_row)
    head_count = parts["query_f"].shape[1]
    grad_f = out_grad[0].astype(jnp.float32).reshape(row_count, head_count, DV)
    first_f = parts["first_id"].astype(jnp.float32)
    last_f = parts["last_id"].astype(jnp.float32)
    neutral = (
        jnp.ones((head_count, DK), jnp.float32),
        jnp.zeros((head_count, DK, DV), jnp.float32),
        jnp.float32(-1.0),
        jnp.float32(-1.0),
    )
    unused_dec, state_in, unused_first, prior_last = prefix(
        (parts["decay_all"], state_end(parts), first_f, last_f), "ctx", join_forward, neutral, False
    )
    use_state = (prior_last == first_f).astype(jnp.float32)
    other_dec, carry_in, next_first, other_last = prefix(
        (parts["decay_all"], start_grad(parts, grad_f), first_f, last_f),
        "ctx",
        join_backward,
        neutral,
        True,
    )
    use_carry = (next_first == last_f).astype(jnp.float32)
    attn_rows, grad_query, grad_key, grad_value, grad_log, sum_start = finish(
        parts, grad_f, state_in, use_state, carry_in, use_carry
    )
    sums_in, later_first, later_last = prefix(
        (sum_start, first_f, last_f),
        "ctx",
        join_sums,
        (jnp.zeros((head_count, DK), jnp.float32), jnp.float32(-1.0), jnp.float32(-1.0)),
        True,
    )
    use_sums = (later_first == last_f).astype(jnp.float32)
    grad_decay = decay_grad_of(parts, grad_log, sums_in, use_sums)
    attn_out = attn_rows.reshape(row_count, head_count * DV).astype(jnp.bfloat16)[None]
    query_back = grad_query.reshape(row_count, head_count * DK).astype(jnp.bfloat16)
    key_back = grad_key.reshape(row_count, head_count * DK).astype(jnp.bfloat16)
    value_back = grad_value.reshape(row_count, head_count * DV).astype(jnp.bfloat16)
    decay_back = grad_decay.reshape(row_count, head_count * DK).astype(jnp.bfloat16)
    gathered_back = (
        lax.all_gather(query_back[None], "dp", axis=0, tiled=True),
        lax.all_gather(key_back[None], "dp", axis=0, tiled=True),
        lax.all_gather(value_back[None], "dp", axis=0, tiled=True),
        lax.all_gather(decay_back[None], "dp", axis=0, tiled=True),
    )
    dest_ids = my_order // per_peer
    dest_slots = dp_index * per_peer + my_order % per_peer
    returned = tuple(
        (
            whole.reshape(dp_count, block_count, BLK, whole.shape[-1])[
                dest_ids, dest_slots
            ].reshape(1, row_count, whole.shape[-1])
            for whole in gathered_back
        )
    )
    query_grad, key_grad, value_grad, decay_grad = returned
    return (attn_out, query_grad, key_grad, value_grad, decay_grad)


def solution(mesh):
    placed = (
        P("dp", "ctx", None),
        P("dp", "ctx", None),
        P("dp", "ctx", None),
        P("dp", "ctx", None),
        P("dp", "ctx", None),
        P("dp", "ctx"),
        P(None, "ctx", None),
    )
    return jax.shard_map(
        body,
        mesh=mesh,
        in_specs=placed,
        out_specs=(
            P("dp", "ctx", None),
            P("dp", "ctx", None),
            P("dp", "ctx", None),
            P("dp", "ctx", None),
            P("dp", "ctx", None),
        ),
        check_vma=False,
    )
```

profile of v0, /device:TPU:0, one launch (start us, length us, event | category | flops | bytes accessed | tf_op | source)
XLA Modules:
  0.0 467.1 jit_solution(8892131721895761153)
XLA Ops:
  10.0 1.3 copy.152
  11.3 0.8 select_reduce_fusion
  12.3 1.3 fusion.43
  13.6 1.8 compare_convert_fusion
  15.5 23.7 %all-gather.18.cloned.1.call-done = bf16[4,128,1024]{2,1,0:T(8,128)(2,1)} async-done(((bf16[1,128,1024]{2,1,0:T(8,128)(2,1)}), bf16[4,128,1024]{2,1,0:T(8,128)(2,1)}) %all-gather.18.cloned.1.call-update) | async-done | bytes 1048592 | tf_op jit(solution)/shard_map/all_gather | solution.py:186
  39.2 1.8 gather_fusion.2
  41.0 1.3 reshape.327
  42.3 1.4 fusion.44
  44.1 23.6 %all-gather.16.cloned.1.call-done = bf16[4,128,1024]{2,1,0:T(8,128)(2,1)} async-done(((bf16[1,128,1024]{2,1,0:T(8,128)(2,1)}), bf16[4,128,1024]{2,1,0:T(8,128)(2,1)}) %all-gather.16.cloned.1.call-update) | async-done | bytes 1048592 | tf_op jit(solution)/shard_map/all_gather | solution.py:183
  67.7 1.8 gather_fusion.1
  69.5 1.3 reshape.326
  70.8 1.6 copy.125
  72.5 1.9 convolution_multiply_fusion.4
  74.6 21.7 %all-gather.20.cloned.1.call-done = bf16[4,128,1024]{2,1,0:T(8,128)(2,1)} async-done(((bf16[1,128,1024]{2,1,0:T(8,128)(2,1)}), bf16[4,128,1024]{2,1,0:T(8,128)(2,1)}) %all-gather.20.cloned.1.call-update) | async-done | bytes 1048592 | tf_op jit(solution)/shard_map/all_gather | solution.py:184
  96.2 1.8 gather_fusion.3
  98.0 1.3 reshape.328
  99.3 1.6 copy.127
  100.9 0.7 slice_exponential_fusion
  101.6 31.6 %all-gather.14.cloned.1.call-done = bf16[4,128,2048]{2,1,0:T(8,128)(2,1)} async-done(((bf16[1,128,2048]{2,1,0:T(8,128)(2,1)}), bf16[4,128,2048]{2,1,0:T(8,128)(2,1)}) %all-gather.14.cloned.1.call-update) | async-done | bytes 2097168 | tf_op jit(solution)/shard_map/all_gather | solution.py:185
  133.3 2.2 gather_fusion
  135.6 1.5 fusion.18
  138.9 0.8 dynamic-update-slice.2
  139.7 0.8 dynamic-update-slice.1
  140.4 17.0 %all-reduce.3 = (f32[8]{0:T(128)S(1)}, f32[8]{0:T(128)S(1)}) all-reduce(f32[8]{0:T(128)S(1)} %dynamic-update-slice.1, f32[8]{0:T(128)S(1)} %dynamic-update-slice.2), channel_id=1, replica_groups=mesh['dp'=4,'ctx'=8] {'ctx'}, use_global_device_ids=true, to_apply=%add.1 | all-reduce | flops 16 | bytes 128
  157.5 14.2 %all_gather.78 = f32[8,16,64]{2,1,0:T(8,128)S(1)} all-gather(f32[1,16,64]{2,1,0:T(8,128)S(1)} %get-tuple-element.421), channel_id=1, replica_groups=mesh['dp'=4,'ctx'=8] {'ctx'}, dimensions={0}, use_global_device_ids=true | all-gather | bytes 36864 | tf_op jit(solution)/shard_map/all_gather | solution.py:16
  171.7 1.6 fusion.6
  173.2 9.4 %all-gather.32.cloned.1.call-done = f32[128,64,128]{2,1,0:T(8,128)} async-done(((f32[16,64,128]{2,1,0:T(8,128)}), f32[128,64,128]{2,1,0:T(8,128)}) %all-gather.32.cloned.1.call-update) | async-done | bytes 4194320 | tf_op jit(solution)/shard_map/all_gather | solution.py:16
  182.6 45.4 %while.51 = (s32[]{:T(128)}, f32[16,64,128]{2,1,0:T(8,128)S(1)}, f32[]{:T(128)}, s32[]{:T(128)}, f32[8,16,64,128]{3,2,1,0:T(8,128)}, /*index=5*/f32[8]{0:T(128)S...) while((s32[]{:T(128)}, f32[16,64,128]{2,1,0:T(8,128)S(1)}, ...), condition=%wide.region_5.6_spmd, body=%wide.region_4.5_spmd.sunk | while | flops 525326 | bytes 1585431 | solution.py:25
  186.4 1.5 bitcast_select_fusion.7
  192.9 1.5 bitcast_select_fusion.7
  199.3 1.5 bitcast_select_fusion.7
  205.8 1.5 bitcast_select_fusion.7
  212.3 1.5 bitcast_select_fusion.7
  218.8 1.5 bitcast_select_fusion.7
  225.3 1.5 bitcast_select_fusion.7
  228.0 2.5 all-gather.30.cloned.1.call-done
  230.6 1.3 compare_select_fusion.3
  232.0 1.1 fusion.16
  233.7 2.2 fusion.12
  235.9 2.1 multiply_reduce_fusion
  238.0 1.2 fusion.34
  239.2 61.9 %all-gather.2 = f32[128,64]{1,0:T(8,128)S(1)} all-gather(f32[16,64]{1,0:T(8,128)S(1)} %get-tuple-element.419), channel_id=4, replica_groups=mesh['dp'=4,'ctx'=8] {'ctx'}, dimensions={0}, use_global_device_ids=true | all-gather | bytes 36864 | tf_op jit(solution)/shard_map/all_gather | solution.py:16
  301.0 34.3 %while.52 = (s32[]{:T(128)}, f32[16,64]{1,0:T(8,128)S(1)}, f32[]{:T(128)}, s32[]{:T(128)}, f32[8,16,64]{2,1,0:T(8,128)S(1)}, /*index=5*/f32[8]{0:T(128)S(1)}, f3...) while((s32[]{:T(128)}, f32[16,64]{1,0:T(8,128)S(1)}, f32[]{:T(128)}, ...), condition=%wide.region_8.9_spmd, body=%wide.region_7.8_spmd.sunk | while | flops 4110 | bytes 12555 | solution.py:25
  335.3 1.2 add_convert_fusion
  336.6 0.8 copy.147
  337.5 1.8 copy.139
  339.4 1.8 copy.136
  341.2 2.9 convolution_multiply_fusion.3
  344.1 1.0 copy-done.4
  345.1 1.0 fusion.5
  346.1 2.8 fusion.9
  349.0 1.3 copy.143
  350.3 1.0 copy.144
  352.0 2.4 fusion.24
  354.4 1.8 fusion.10
  356.3 1.0 copy.148
  357.3 5.4 %all-gather.28.cloned.1.call-done = bf16[4,128,1024]{2,1,0:T(8,128)(2,1)} async-done(((bf16[1,128,1024]{2,1,0:T(8,128)(2,1)}), bf16[4,128,1024]{2,1,0:T(8,128)(2,1)}) %all-gather.28.cloned.1.call-update) | async-done | bytes 1048592 | tf_op jit(solution)/shard_map/all_gather | solution.py:246
  362.6 2.5 gather_fusion.7
  365.1 26.0 %all-gather.24.cloned.1.call-done = bf16[4,128,1024]{2,1,0:T(8,128)(2,1)} async-done(((bf16[1,128,1024]{2,1,0:T(8,128)(2,1)}), bf16[4,128,1024]{2,1,0:T(8,128)(2,1)}) %all-gather.24.cloned.1.call-update) | async-done | bytes 1048592 | tf_op jit(solution)/shard_map/all_gather | solution.py:244
  391.1 2.5 gather_fusion.5
  393.6 26.6 %all-gather.22.cloned.1.call-done = bf16[4,128,1024]{2,1,0:T(8,128)(2,1)} async-done(((bf16[1,128,1024]{2,1,0:T(8,128)(2,1)}), bf16[4,128,1024]{2,1,0:T(8,128)(2,1)}) %all-gather.22.cloned.1.call-update) | async-done | bytes 1048592 | tf_op jit(solution)/shard_map/all_gather | solution.py:243
  420.2 2.5 gather_fusion.4
  422.7 34.5 %all-gather.26.cloned.1.call-done = bf16[4,128,2048]{2,1,0:T(8,128)(2,1)} async-done(((bf16[1,128,2048]{2,1,0:T(8,128)(2,1)}), bf16[4,128,2048]{2,1,0:T(8,128)(2,1)}) %all-gather.26.cloned.1.call-update) | async-done | bytes 2097168 | tf_op jit(solution)/shard_map/all_gather | solution.py:245
  457.3 3.0 gather_fusion.6
  (99 shorter events, 23.0 us)
Async XLA Ops:
  7.2 32.0 %all-gather.18.cloned.1.call-start = ((), (), s32[]{:S(2)}) async-start(), calls=%async_computation.2 | async-start | bytes 1310720 | tf_op jit(solution)/shard_map/all_gather | solution.py:186
  7.9 59.8 %all-gather.16.cloned.1.call-start = ((), (), s32[]{:S(2)}) async-start(), calls=%async_computation.1 | async-start | bytes 1310720 | tf_op jit(solution)/shard_map/all_gather | solution.py:183
  8.6 87.6 %all-gather.20.cloned.1.call-start = ((), (), s32[]{:S(2)}) async-start(), calls=%async_computation.3 | async-start | bytes 1310720 | tf_op jit(solution)/shard_map/all_gather | solution.py:184
  9.4 123.9 %all-gather.14.cloned.1.call-start = ((), (), s32[]{:S(2)}) async-start(), calls=%async_computation | async-start | bytes 2621440 | tf_op jit(solution)/shard_map/all_gather | solution.py:185
  10.0 172.6 %all-gather.32.cloned.1.call-start = ((), (), s32[]{:S(2)}) async-start(), calls=%async_computation.9 | async-start | bytes 4718592 | tf_op jit(solution)/shard_map/all_gather | solution.py:16
  43.7 25.8 %copy-start.7 = (f32[128,16,64]{2,1,0:T(8,128)}, f32[128,16,64]{2,1,0:T(8,128)S(1)}, u32[]{:S(2)}) copy-start(f32[128,16,64]{2,1,0:T(8,128)S(1)} %fusion.44) | copy-start | bytes 1572868
  72.4 25.6 %copy-start.5 = (f32[128,16,64]{0,2,1:T(8,128)}, f32[128,16,64]{0,2,1:T(8,128)S(1)}, u32[]{:S(2)}) copy-start(f32[128,16,64]{0,2,1:T(8,128)S(1)} %copy.125) | copy-start | bytes 1572868
  72.5 62.9 %copy-start = (f32[128,16,64]{0,2,1:T(8,128)}, f32[128,16,64]{0,2,1:T(8,128)S(1)}, u32[]{:S(2)}) copy-start(f32[128,16,64]{0,2,1:T(8,128)S(1)} %exponential_multiply_fusion) | copy-start | bytes 1572868
  74.5 63.8 %copy-start.9 = (u32[32]{0:T(128)S(1)}, u32[32]{0:T(128)}, u32[]{:S(2)}) copy-start(u32[32]{0:T(128)} %constant.302) | copy-start | bytes 388
  74.5 82.9 %copy-start.8 = (s32[1,128]{1,0:T(1,128)S(1)}, s32[1,128]{1,0:T(1,128)}, u32[]{:S(2)}) copy-start(s32[1,128]{1,0:T(1,128)} %param.18) | copy-start | bytes 1540
  74.5 156.0 %all-gather.30.cloned.1.call-start = ((), (), s32[]{:S(2)}) async-start(), calls=%async_computation.8 | async-start | bytes 4718592 | tf_op jit(solution)/shard_map/all_gather | solution.py:16
  137.1 225.6 %all-gather.28.cloned.1.call-start = ((), (), s32[]{:S(2)}) async-start(), calls=%async_computation.7 | async-start | bytes 1310720 | tf_op jit(solution)/shard_map/all_gather | solution.py:246
  230.6 3.1 copy-start.3
  230.6 5.2 %copy-start.1 = (f32[128,16,64]{0,2,1:T(8,128)S(1)}, f32[128,16,64]{0,2,1:T(8,128)}, u32[]{:S(2)}) copy-start(f32[128,16,64]{0,2,1:T(8,128)} %copy-done) | copy-start | bytes 1572868
  230.6 5.2 %copy-start.6 = (f32[128,16,64]{0,2,1:T(8,128)S(1)}, f32[128,16,64]{0,2,1:T(8,128)}, u32[]{:S(2)}) copy-start(f32[128,16,64]{0,2,1:T(8,128)} %copy-done.5) | copy-start | bytes 1572868
  337.4 53.7 %all-gather.24.cloned.1.call-start = ((), (), s32[]{:S(2)}) async-start(), calls=%async_computation.5 | async-start | bytes 1310720 | tf_op jit(solution)/shard_map/all_gather | solution.py:244
  339.3 80.9 %all-gather.22.cloned.1.call-start = ((), (), s32[]{:S(2)}) async-start(), calls=%async_computation.4 | async-start | bytes 1310720 | tf_op jit(solution)/shard_map/all_gather | solution.py:243
  341.2 116.1 %all-gather.26.cloned.1.call-start = ((), (), s32[]{:S(2)}) async-start(), calls=%async_computation.6 | async-start | bytes 2621440 | tf_op jit(solution)/shard_map/all_gather | solution.py:245
  344.1 1.0 copy-start.4
  346.1 8.3 %copy-start.2 = (f32[128,16,64]{0,2,1:T(8,128)S(1)}, f32[128,16,64]{0,2,1:T(8,128)}, u32[]{:S(2)}) copy-start(f32[128,16,64]{0,2,1:T(8,128)} %copy-done) | copy-start | bytes 1572868
Sparse Core Ops, SparseCore 0:
  9.8 29.3 all-gather.17
  41.0 26.6 all-gather.15
  69.6 26.6 all-gather.19
  97.9 35.2 all-gather.13
  134.7 47.8 all-gather.31
  184.6 45.8 all-gather.29
  337.6 25.0 all-gather.27
  364.5 26.6 all-gather.23
  393.6 26.6 all-gather.21
  421.9 35.2 all-gather.25
where the time goes:
time: 469 us; the launch traced here: 467 us
  waiting for transfers between devices  208 us (44%)
  blocking collectives  93 us (20%)
  local copies, waits for them, and re-layouts  57.1 us (12%)
  loops' own time  52.2 us (11%)
  matrix products  23.1 us (5%)
  other arithmetic  18 us (4%)
  between operations  15.7 us (3%)
    all_gather x2, blocking collectives, prefix(): gathered = jax.tree.map(lambda a: lax.all_gather(a, axis), part)  76 us
    another operation x3, loops' own time, prefix(): return lax.fori_loop(0, ahead, one, state)  52.2 us
    all_gather x1, waiting for transfers between devices, body(): lax.all_gather(value_back[None], 'dp', axis=0, tiled=True)  34.5 us
    all_gather x1, waiting for transfers between devices, body(): lax.all_gather(value_rows, 'dp', axis=0, tiled=True)  31.6 us
    all_gather x1, waiting for transfers between devices, body(): lax.all_gather(query_back[None], 'dp', axis=0, tiled=True)  26.6 us
    all_gather x1, waiting for transfers between devices, body(): lax.all_gather(key_back[None], 'dp', axis=0, tiled=True)  26 us
    all_gather x1, waiting for transfers between devices, body(): lax.all_gather(log_decay, 'dp', axis=0, tiled=True)  23.7 us
    all_gather x1, waiting for transfers between devices, body(): lax.all_gather(query_rows, 'dp', axis=0, tiled=True)  23.6 us
  transfers between devices with their start and end apart: 10, of which 10 were waited for; matrix products, arithmetic and copies ran while one was open for 16% of the time, Pallas kernels for 0%

commit v1 on v0

--- a/solution.py
+++ b/solution.py
@@ -7,6 +7,27 @@
 DV = 128
 BLK = 32
 HIGH = lax.Precision.HIGHEST
+
+
+def ring_gather(x, axis, dim):
+    peers, index, extent = (lax.axis_size(axis), lax.axis_index(axis), x.shape[dim])
+    forward = [(i, (i + 1) % peers) for i in range(peers)]
+    downward = [(i, (i - 1) % peers) for i in range(peers)]
+    out = jnp.zeros((*x.shape[:dim], peers * extent, *x.shape[dim + 1 :]), x.dtype)
+    out = lax.dynamic_update_slice_in_dim(out, x, index * extent, axis=dim)
+    from_left = from_right = x
+    halfway = peers // 2
+    for turn in range(1, halfway + 1):
+        from_left = lax.ppermute(from_left, axis, forward)
+        out = lax.dynamic_update_slice_in_dim(
+            out, from_left, (index - turn) % peers * extent, axis=dim
+        )
+        if turn < peers - halfway:
+            from_right = lax.ppermute(from_right, axis, downward)
+            out = lax.dynamic_update_slice_in_dim(
+                out, from_right, (index + turn) % peers * extent, axis=dim
+            )
+    return out
 
 
 def prefix(part, axis, combine, identity, reverse):
@@ -240,7 +261,7 @@
     value_back = grad_value.reshape(row_count, head_count * DV).astype(jnp.bfloat16)
     decay_back = grad_decay.reshape(row_count, head_count * DK).astype(jnp.bfloat16)
     gathered_back = (
-        lax.all_gather(query_back[None], "dp", axis=0, tiled=True),
+        ring_gather(query_back[None], "dp", 0),
         lax.all_gather(key_back[None], "dp", axis=0, tiled=True),
         lax.all_gather(value_back[None], "dp", axis=0, tiled=True),
         lax.all_gather(decay_back[None], "dp", axis=0, tiled=True),

time: 469 us -> 444 us (0.947)
  waiting for transfers between devices: 208 us -> 159 us
  other arithmetic: 18 us -> 39.9 us
  starting transfers between devices: 0.4 us -> 5.52 us
    all_gather x1 -> x0, waiting for transfers between devices: 26.6 us -> none  [body(): lax.all_gather(query_back[None], 'dp', axis=0, tiled=True)]
    another operation x1, other arithmetic: 1.36 us -> 23.3 us  [prepare(): jnp.cumsum(decay_b.astype(jnp.float32).reshape(row_count, head_count, DK)...]
    all_gather x1, waiting for transfers between devices: 23.6 us -> 2.68 us  [body(): lax.all_gather(query_rows, 'dp', axis=0, tiled=True)]
    ppermute x0 -> x3, waiting for transfers between devices: none -> 13.7 us  [the longest x2 12.4 us: ring_gather(): from_left = lax.ppermute(from_left, axis, forward)]
    all_gather x1, waiting for transfers between devices: 26 us -> 16.4 us  [body(): lax.all_gather(key_back[None], 'dp', axis=0, tiled=True)]
    all_gather x1, waiting for transfers between devices: 5.38 us -> 0.01 us  [body(): lax.all_gather(decay_back[None], 'dp', axis=0, tiled=True)]
    ppermute x0 -> x3, starting transfers between devices: none -> 5.16 us  [the longest x2 3.58 us: ring_gather(): from_left = lax.ppermute(from_left, axis, forward)]
  transfers between devices with their start and end apart: 10 -> 12, of which waited for: 10 -> 11; matrix products, arithmetic and copies ran while one was open for 16% -> 21% of each run, Pallas kernels for 0% -> 0%
where the time goes in v1:
time: 444 us; the launch traced here: 442 us
  waiting for transfers between devices  159 us (36%)
  blocking collectives  93 us (21%)
  local copies, waits for them, and re-layouts  53.6 us (12%)
  loops' own time  52.2 us (12%)
  other arithmetic  39.9 us (9%)
  matrix products  23.1 us (5%)
  between operations  15.5 us (3%)
  starting transfers between devices  5.52 us (1%)
    all_gather x2, blocking collectives, prefix(): gathered = jax.tree.map(lambda a: lax.all_gather(a, axis), part)  76 us
    another operation x3, loops' own time, prefix(): return lax.fori_loop(0, ahead, one, state)  52.2 us
    all_gather x1, waiting for transfers between devices, body(): lax.all_gather(value_back[None], 'dp', axis=0, tiled=True)  34.7 us
    all_gather x1, waiting for transfers between devices, body(): lax.all_gather(value_rows, 'dp', axis=0, tiled=True)  32.3 us
    all_gather x1, waiting for transfers between devices, body(): lax.all_gather(log_decay, 'dp', axis=0, tiled=True)  23.7 us
    another operation x1, other arithmetic, prepare(): jnp.cumsum(decay_b.astype(jnp.float32).reshape(row_count, head_count, DK)...  23.3 us
    all_gather x1, waiting for transfers between devices, body(): lax.all_gather(key_rows, 'dp', axis=0, tiled=True)  20.8 us
    unnamed x1, blocking collectives  17 us
  transfers between devices with their start and end apart: 12, of which 11 were waited for; matrix products, arithmetic and copies ran while one was open for 21% of the time, Pallas kernels for 0%

profile of v1, /device:TPU:0, one launch (start us, length us, event | category | flops | bytes accessed | tf_op | source)
XLA Modules:
  0.0 441.7 jit_solution(8101787578206000379)
XLA Ops:
  10.0 1.3 copy.162
  11.3 0.8 select_reduce_fusion
  12.3 1.3 fusion.40
  13.6 1.8 compare_convert_fusion
  15.5 23.7 %all-gather.17.cloned.1.call-done = bf16[4,128,1024]{2,1,0:T(8,128)(2,1)} async-done(((bf16[1,128,1024]{2,1,0:T(8,128)(2,1)}), bf16[4,128,1024]{2,1,0:T(8,128)(2,1)}) %all-gather.17.cloned.1.call-update) | async-done | bytes 1048592 | tf_op jit(solution)/shard_map/all_gather | solution.py:207
  39.2 1.8 gather_fusion.2
  41.3 23.3 %fusion.41 = f32[128,16,64]{2,1,0:T(8,128)S(1)} fusion(f32[128,16,64]{2,1,0:T(8,128)S(1)} %reshape.327), kind=kOutput, calls=%fused_computation.88 | output fusion | flops 16646144 | bytes 1048576 | tf_op jit(solution)/shard_map/jit(cumsum)/reduce_window_sum | solution.py:55
  65.0 2.7 all-gather.15.cloned.1.call-done
  67.7 1.8 gather_fusion.1
  69.5 1.3 reshape.326
  70.8 1.6 copy.133
  72.5 0.9 copy-done
  73.4 1.9 convolution_multiply_fusion.4
  75.4 20.8 %all-gather.19.cloned.1.call-done = bf16[4,128,1024]{2,1,0:T(8,128)(2,1)} async-done(((bf16[1,128,1024]{2,1,0:T(8,128)(2,1)}), bf16[4,128,1024]{2,1,0:T(8,128)(2,1)}) %all-gather.19.cloned.1.call-update) | async-done | bytes 1048592 | tf_op jit(solution)/shard_map/all_gather | solution.py:205
  96.2 1.8 gather_fusion.3
  98.0 1.3 reshape.328
  99.3 1.6 copy.135
  100.9 32.3 %all-gather.13.cloned.1.call-done = bf16[4,128,2048]{2,1,0:T(8,128)(2,1)} async-done(((bf16[1,128,2048]{2,1,0:T(8,128)(2,1)}), bf16[4,128,2048]{2,1,0:T(8,128)(2,1)}) %all-gather.13.cloned.1.call-update) | async-done | bytes 2097168 | tf_op jit(solution)/shard_map/all_gather | solution.py:206
  133.3 2.2 gather_fusion
  135.6 1.5 fusion.18
  140.4 17.0 %all-reduce.3 = (f32[8]{0:T(128)S(1)}, f32[8]{0:T(128)S(1)}) all-reduce(f32[8]{0:T(128)S(1)} %dynamic-update-slice.1, f32[8]{0:T(128)S(1)} %dynamic-update-slice.2), channel_id=1, replica_groups=mesh['dp'=4,'ctx'=8] {'ctx'}, use_global_device_ids=true, to_apply=%add.1 | all-reduce | flops 16 | bytes 128
  157.5 14.2 %all_gather.75 = f32[8,16,64]{2,1,0:T(8,128)S(1)} all-gather(f32[1,16,64]{2,1,0:T(8,128)S(1)} %get-tuple-element.421), channel_id=1, replica_groups=mesh['dp'=4,'ctx'=8] {'ctx'}, dimensions={0}, use_global_device_ids=true | all-gather | bytes 36864 | tf_op jit(solution)/shard_map/all_gather | solution.py:37
  171.7 1.6 fusion.6
  173.2 9.4 %all-gather.29.cloned.1.call-done = f32[128,64,128]{2,1,0:T(8,128)} async-done(((f32[16,64,128]{2,1,0:T(8,128)}), f32[128,64,128]{2,1,0:T(8,128)}) %all-gather.29.cloned.1.call-update) | async-done | bytes 4194320 | tf_op jit(solution)/shard_map/all_gather | solution.py:37
  182.6 45.4 %while.51 = (s32[]{:T(128)}, f32[16,64,128]{2,1,0:T(8,128)S(1)}, f32[]{:T(128)}, s32[]{:T(128)}, f32[8,16,64,128]{3,2,1,0:T(8,128)}, /*index=5*/f32[8]{0:T(128)S...) while((s32[]{:T(128)}, f32[16,64,128]{2,1,0:T(8,128)S(1)}, ...), condition=%wide.region_5.6_spmd, body=%wide.region_4.5_spmd.sunk | while | flops 525326 | bytes 1585431 | solution.py:46
  186.4 1.5 bitcast_select_fusion.7
  192.9 1.5 bitcast_select_fusion.7
  199.4 1.5 bitcast_select_fusion.7
  205.8 1.5 bitcast_select_fusion.7
  212.3 1.5 bitcast_select_fusion.7
  218.8 1.5 bitcast_select_fusion.7
  225.3 1.5 bitcast_select_fusion.7
  228.0 2.5 all-gather.27.cloned.1.call-done
  230.6 1.3 compare_select_fusion.3
  232.0 1.1 fusion.16
  233.7 2.2 fusion.12
  235.9 2.1 multiply_reduce_fusion
  238.0 1.2 fusion.34
  239.2 61.8 %all-gather.2 = f32[128,64]{1,0:T(8,128)S(1)} all-gather(f32[16,64]{1,0:T(8,128)S(1)} %get-tuple-element.419), channel_id=4, replica_groups=mesh['dp'=4,'ctx'=8] {'ctx'}, dimensions={0}, use_global_device_ids=true | all-gather | bytes 36864 | tf_op jit(solution)/shard_map/all_gather | solution.py:37
  301.0 34.3 %while.52 = (s32[]{:T(128)}, f32[16,64]{1,0:T(8,128)S(1)}, f32[]{:T(128)}, s32[]{:T(128)}, f32[8,16,64]{2,1,0:T(8,128)S(1)}, /*index=5*/f32[8]{0:T(128)S(1)}, f3...) while((s32[]{:T(128)}, f32[16,64]{1,0:T(8,128)S(1)}, f32[]{:T(128)}, ...), condition=%wide.region_8.9_spmd, body=%wide.region_7.8_spmd.sunk | while | flops 4110 | bytes 12555 | solution.py:46
  335.3 1.2 add_convert_fusion
  336.6 0.9 copy.157
  337.5 1.8 copy.149
  339.4 2.9 convolution_multiply_fusion.3
  342.3 1.0 copy-done.4
  343.3 1.0 fusion.5
  344.3 2.8 fusion.9
  347.2 1.3 copy.153
  348.5 1.0 copy.154
  350.3 2.4 fusion.24
  352.8 1.4 collective-permute-start
  354.2 1.6 collective-permute-start.1
  355.8 1.8 fusion.10
  357.6 9.1 %collective-permute-done = bf16[1,128,1024]{2,1,0:T(8,128)(2,1)S(1)} collective-permute-done((bf16[1,128,1024]{2,1,0:T(8,128)(2,1)S(1)}, bf16[1,128,1024]{2,1,0:T(8,128)(2,1)S(1)}, u32[]{:S(2)}, u32[]{:S(2)}) %collective-permute-start) | collective-permute-done | bytes 262176 | tf_op jit(solution)/shard_map/ppermute | solution.py:21
  366.7 2.2 collective-permute-start.2
  369.1 1.0 copy.158
  370.1 1.2 collective-permute-done.1
  371.4 3.3 collective-permute-done.2
  374.8 1.3 gather_fusion.4
  376.0 2.5 gather_fusion.7
  378.5 16.4 %all-gather.21.cloned.1.call-done = bf16[4,128,1024]{2,1,0:T(8,128)(2,1)} async-done(((bf16[1,128,1024]{2,1,0:T(8,128)(2,1)}), bf16[4,128,1024]{2,1,0:T(8,128)(2,1)}) %all-gather.21.cloned.1.call-update) | async-done | bytes 1048592 | tf_op jit(solution)/shard_map/all_gather | solution.py:265
  395.0 2.5 gather_fusion.5
  397.5 34.7 %all-gather.23.cloned.1.call-done = bf16[4,128,2048]{2,1,0:T(8,128)(2,1)} async-done(((bf16[1,128,2048]{2,1,0:T(8,128)(2,1)}), bf16[4,128,2048]{2,1,0:T(8,128)(2,1)}) %all-gather.23.cloned.1.call-update) | async-done | bytes 2097168 | tf_op jit(solution)/shard_map/all_gather | solution.py:266
  432.2 3.0 gather_fusion.6
  (107 shorter events, 25.1 us)
Async XLA Ops:
  7.2 32.0 %all-gather.17.cloned.1.call-start = ((), (), s32[]{:S(2)}) async-start(), calls=%async_computation.2 | async-start | bytes 1310720 | tf_op jit(solution)/shard_map/all_gather | solution.py:207
  7.9 59.8 %all-gather.15.cloned.1.call-start = ((), (), s32[]{:S(2)}) async-start(), calls=%async_computation.1 | async-start | bytes 1310720 | tf_op jit(solution)/shard_map/all_gather | solution.py:204
  8.6 87.6 %all-gather.19.cloned.1.call-start = ((), (), s32[]{:S(2)}) async-start(), calls=%async_computation.3 | async-start | bytes 1310720 | tf_op jit(solution)/shard_map/all_gather | solution.py:205
  9.4 123.9 %all-gather.13.cloned.1.call-start = ((), (), s32[]{:S(2)}) async-start(), calls=%async_computation | async-start | bytes 2621440 | tf_op jit(solution)/shard_map/all_gather | solution.py:206
  10.0 172.6 %all-gather.29.cloned.1.call-start = ((), (), s32[]{:S(2)}) async-start(), calls=%async_computation.8 | async-start | bytes 4718592 | tf_op jit(solution)/shard_map/all_gather | solution.py:37
  72.4 63.0 %copy-start.5 = (f32[128,16,64]{0,2,1:T(8,128)}, f32[128,16,64]{0,2,1:T(8,128)S(1)}, u32[]{:S(2)}) copy-start(f32[128,16,64]{0,2,1:T(8,128)S(1)} %copy.133) | copy-start | bytes 1572868
  72.5 0.9 copy-start
  75.3 63.0 %copy-start.9 = (u32[32]{0:T(128)S(1)}, u32[32]{0:T(128)}, u32[]{:S(2)}) copy-start(u32[32]{0:T(128)} %constant.328) | copy-start | bytes 388
  75.3 82.1 %copy-start.8 = (s32[1,128]{1,0:T(1,128)S(1)}, s32[1,128]{1,0:T(1,128)}, u32[]{:S(2)}) copy-start(s32[1,128]{1,0:T(1,128)} %param.18) | copy-start | bytes 1540
  75.3 155.2 %all-gather.27.cloned.1.call-start = ((), (), s32[]{:S(2)}) async-start(), calls=%async_computation.7 | async-start | bytes 4718592 | tf_op jit(solution)/shard_map/all_gather | solution.py:37
  137.1 239.0 %all-gather.25.cloned.1.call-start = ((), (), s32[]{:S(2)}) async-start(), calls=%async_computation.6 | async-start | bytes 1310720 | tf_op jit(solution)/shard_map/all_gather | solution.py:267
  230.6 3.1 copy-start.3
  230.6 5.2 %copy-start.1 = (f32[128,16,64]{0,2,1:T(8,128)S(1)}, f32[128,16,64]{0,2,1:T(8,128)}, u32[]{:S(2)}) copy-start(f32[128,16,64]{0,2,1:T(8,128)} %copy-done) | copy-start | bytes 1572868
  230.6 5.2 %copy-start.6 = (f32[128,16,64]{0,2,1:T(8,128)S(1)}, f32[128,16,64]{0,2,1:T(8,128)}, u32[]{:S(2)}) copy-start(f32[128,16,64]{0,2,1:T(8,128)} %copy-done.5) | copy-start | bytes 1572868
  337.5 57.5 %all-gather.21.cloned.1.call-start = ((), (), s32[]{:S(2)}) async-start(), calls=%async_computation.4 | async-start | bytes 1310720 | tf_op jit(solution)/shard_map/all_gather | solution.py:265
  339.3 92.8 %all-gather.23.cloned.1.call-start = ((), (), s32[]{:S(2)}) async-start(), calls=%async_computation.5 | async-start | bytes 2621440 | tf_op jit(solution)/shard_map/all_gather | solution.py:266
  342.3 1.0 copy-start.4
  344.3 8.3 %copy-start.7 = (bf16[128,16,64]{0,2,1:T(8,128)(2,1)S(1)}, bf16[128,16,64]{0,2,1:T(8,128)(2,1)}, u32[]{:S(2)}) copy-start(bf16[128,16,64]{0,2,1:T(8,128)(2,1)} %get-tuple-element.423) | copy-start | bytes 786436
  344.3 11.5 %copy-start.2 = (f32[128,16,64]{0,2,1:T(8,128)S(1)}, f32[128,16,64]{0,2,1:T(8,128)}, u32[]{:S(2)}) copy-start(f32[128,16,64]{0,2,1:T(8,128)} %copy-done) | copy-start | bytes 1572868
  352.8 13.9 %collective-permute-start = (bf16[1,128,1024]{2,1,0:T(8,128)(2,1)S(1)}, bf16[1,128,1024]{2,1,0:T(8,128)(2,1)S(1)}, u32[]{:S(2)}, u32[]{:S(2)}) collective-permute-start(bf16[1,128,1024]{2,1,0:T(8,128)(2,1)S(1)} %copy.144), channel_id=1, source_target_pairs={{0,8},{8,16},{16,24},{24,0},{1,9},{9,17},{17,25},{25,1},{2,10},{10... | collective-permute-start | bytes 786440 | tf_op jit(solution)/shard_map/ppermute | solution.py:21
  354.2 17.1 %collective-permute-start.1 = (bf16[1,128,1024]{2,1,0:T(8,128)(2,1)S(1)}, bf16[1,128,1024]{2,1,0:T(8,128)(2,1)S(1)}, u32[]{:S(2)}, u32[]{:S(2)}) collective-permute-start(bf16[1,128,1024]{2,1,0:T(8,128)(2,1)S(1)} %copy.144), channel_id=1, source_target_pairs={{0,24},{8,0},{16,8},{24,16},{1,25},{9,1},{17,9},{25,17},{2,26},{10... | collective-permute-start | bytes 786440 | tf_op jit(solution)/shard_map/ppermute | solution.py:26
  366.7 8.0 %collective-permute-start.2 = (bf16[1,128,1024]{2,1,0:T(8,128)(2,1)S(1)}, bf16[1,128,1024]{2,1,0:T(8,128)(2,1)S(1)}, u32[]{:S(2)}, u32[]{:S(2)}) collective-permute-start(bf16[1,128,1024]{2,1,0:T(8,128)(2,1)S(1)} %collective-permute-done), channel_id=1, source_target_pairs={{0,8},{8,16},{16,24},{24,0},{1,9},{9,17},{17,25},{25,1},{2,10},{10... | collective-permute-start | bytes 786440 | tf_op jit(solution)/shard_map/ppermute | solution.py:21
Sparse Core Ops, SparseCore 0:
  9.8 29.3 all-gather.16
  41.0 26.6 all-gather.14
  69.6 26.6 all-gather.18
  97.9 35.2 all-gather.12
  134.7 47.8 all-gather.28
  184.6 45.8 all-gather.26
  337.6 31.5 all-gather.24
  371.0 23.9 all-gather.20
  396.8 35.2 all-gather.22
